TPU v7x, 32 devices: a whole 2x2x4 slice. The times are simulated.
32 devices in a mesh: grp: 4 (over y, core), span: 8 (over z, x).
Axes of the slice: x: 2, y: 2, z: 4, core: 2. Of those that a mesh axis runs over, the one named last changes fastest.
Arguments:
- record: float32 [131072, 128], P(('grp', 'span')), may hold values from -96 to 96, as said below
Outputs:
- triangle: float32 [512, 512], replicated
- operator: float32 [512, 512], replicated
Inputs may be any that keep to these rules, and one draw needn't show every extreme that they name: `record`: Real-valued probe samples.
All inputs are finite; a program needn't handle non-finite values.
Results may differ from a plain program's by a relative error of at most 0.0003.
Values sent between devices are 32-bit elements; how exact they have to be, the bound alone decides.
A program may use at most 64 MiB of HBM per device.

v0:
```python
import jax
import jax.numpy as jnp
from jax import lax
from jax.sharding import PartitionSpec as P

LAGS = 4
DELAY = 1024


def shifted(value, axis, steps):
    count = lax.axis_size(axis)
    leading, last = (max(0, -steps), min(count, count - steps))
    return lax.ppermute(value, axis, [(source, source + steps) for source in range(leading, last)])


def inner_rows(left, right):
    return lax.dot_general(
        left,
        right,
        (((0,), (0,)), ((), ())),
        precision=lax.Precision.HIGHEST,
        preferred_element_type=jnp.float32,
    )


def on_device(record):
    count = record.shape[0]
    lead = (LAGS - 1) * DELAY + 1
    following = shifted(record[:lead], ("grp", "span"), -1)
    ext = jnp.concatenate([record, following], 0)
    hank = jnp.concatenate([ext[k * DELAY : k * DELAY + count + 1] for k in range(LAGS)], 1)
    devices = lax.axis_size(("grp", "span"))
    last_row = count * devices - lead
    times = lax.axis_index(("grp", "span")) * count + jnp.arange(count, dtype=jnp.int32)
    weight = (
        jnp.where(times < last_row, 1.0, 0.0)
        - 0.5 * jnp.where(times == 0, 1.0, 0.0)
        - 0.5 * jnp.where(times == last_row, 1.0, 0.0)
    )
    weight = weight.astype(jnp.float32)
    inside = jnp.where(times < last_row, 1.0, 0.0).astype(jnp.float32)
    head = hank[:count]
    weighted = head * weight[:, None]
    cross = inner_rows(head * inside[:, None], hank[1 : count + 1])
    scale = 1.0 / last_row
    gram = inner_rows(weighted, head)
    gram, cross = lax.psum((gram, cross), ("grp", "span"))
    lower = jnp.linalg.cholesky(gram * scale)
    middle = jax.scipy.linalg.solve_triangular(lower, cross * scale, lower=True)
    operator = jax.scipy.linalg.solve_triangular(lower, middle.T, lower=True).T
    return (lower.T, operator)


def solution(mesh):
    placed = (P(("grp", "span"), None),)
    return jax.shard_map(
        on_device, mesh=mesh, in_specs=placed, out_specs=(P(), P()), check_vma=False
    )
```

profile of v0, /device:TPU:0, one launch (start us, length us, event | category | flops | bytes accessed | tf_op | source)
XLA Modules:
  0.0 379.2 jit_solution(13203362706034608490)
XLA Ops:
  7.2 1.5 slice.124
  8.7 1.3 collective-permute-start
  10.0 1.7 constant_dynamic-update-slice_fusion.1
  11.8 36.3 %collective-permute-done = f32[3073,128]{1,0:T(8,128)S(1)} collective-permute-done((f32[3073,128]{1,0:T(8,128)S(1)}, f32[3073,128]{1,0:T(8,128)S(1)}, u32[]{:S(2)}, u32[]{:S(2)}) %collective-permute-start) | collective-permute-done | bytes 1573408 | tf_op jit(solution)/shard_map/ppermute | solution.py:13
  48.1 0.1 constant_dynamic-update-slice_fusion
  48.2 0.5 fusion.64
  48.7 1.4 pad_maximum_fusion
  50.1 17.3 %fusion.2 = f32[512,512]{0,1:T(8,128)} fusion(f32[4097,512]{1,0:T(8,128)S(1)} %pad_maximum_fusion, f32[4096]{0:T(1024)S(1)} %get-tuple-element.52), kind=kOutput, calls=%fused_computation.5 | convolution fusion | flops 12886999040 | bytes 17842176 | tf_op jit(solution)/shard_map/dot_general | solution.py:17
  67.4 16.4 %fusion = f32[512,512]{0,1:T(8,128)} fusion(f32[4097,512]{1,0:T(8,128)S(1)} %pad_maximum_fusion, f32[4096]{0:T(1024)S(1)} %get-tuple-element.51), kind=kOutput, calls=%fused_computation.2 | convolution fusion | flops 12886999040 | bytes 17842176 | tf_op jit(solution)/shard_map/dot_general | solution.py:17
  83.8 139.5 %all-reduce.4.cloned.1.call-done = (f32[512,512]{0,1:T(8,128)}, f32[512,512]{0,1:T(8,128)}) async-done(((f32[512,512]{0,1:T(8,128)}, f32[512,512]{0,1:T(8,128)}), (f32[512,512]{0,1:T(8,128)}, f32[512,512]{0,1:T(8,128)})) %all-reduce.4.cloned.1.call-update) | async-done | bytes 2097168 | tf_op jit(solution)/shard_map/psum | solution.py:47
  223.3 1.3 broadcast_multiply_fusion.1
  224.6 0.3 copy.4
  225.0 1.5 fusion.9
  226.5 11.7 %cholesky.104 = f32[128,128]{1,0:T(8,128)S(1)} custom-call(f32[128,128]{1,0:T(8,128)S(1)} %cholesky.266), custom_call_target="Cholesky" | custom-call | tf_op jit(solution)/shard_map/jit(cholesky)/cholesky | solution.py:48
  238.2 9.8 %custom-call.30 = f32[1,128,128]{1,2,0:T(8,128)S(1)} custom-call(f32[1,128,128]{2,1,0:T(8,128)S(1)} %get-tuple-element.48), custom_call_target="InvertDiagBlocksLowerTriangular" | custom-call | tf_op jit(solution)/shard_map/jit(cholesky)/cholesky | solution.py:48
  248.0 0.1 cholesky.224
  248.1 0.3 constant_dynamic-update-slice_fusion.5
  248.5 0.3 convolution_subtract_fusion.6
  248.8 12.2 %cholesky.217 = f32[128,128]{1,0:T(8,128)S(1)} custom-call(f32[128,128]{1,0:T(8,128)S(1)} %cholesky.270), custom_call_target="Cholesky" | custom-call | tf_op jit(solution)/shard_map/jit(cholesky)/cholesky | solution.py:48
  261.0 0.6 compare_reduce_fusion.2
  261.7 0.6 compare_reduce_fusion.3
  262.3 9.8 %custom-call.31 = f32[1,128,128]{1,2,0:T(8,128)S(1)} custom-call(f32[1,128,128]{2,1,0:T(8,128)S(1)} %get-tuple-element.45), custom_call_target="InvertDiagBlocksLowerTriangular" | custom-call | tf_op jit(solution)/shard_map/jit(cholesky)/cholesky | solution.py:48
  272.1 0.3 convolution_dynamic-update-slice_fusion
  272.4 0.4 convolution_subtract_fusion.7
  272.8 11.7 %cholesky.238 = f32[128,128]{1,0:T(8,128)S(1)} custom-call(f32[128,128]{1,0:T(8,128)S(1)} %cholesky.275), custom_call_target="Cholesky" | custom-call | tf_op jit(solution)/shard_map/jit(cholesky)/cholesky | solution.py:48
  284.5 0.7 compare_reduce_fusion.1
  285.2 9.8 %custom-call.32 = f32[1,128,128]{1,2,0:T(8,128)S(1)} custom-call(f32[1,128,128]{2,1,0:T(8,128)S(1)} %get-tuple-element.42), custom_call_target="InvertDiagBlocksLowerTriangular" | custom-call | tf_op jit(solution)/shard_map/jit(cholesky)/cholesky | solution.py:48
  295.1 0.2 convolution_dynamic-update-slice_fusion.1
  295.3 0.4 convolution_subtract_fusion.8
  295.7 11.9 %cholesky.255 = f32[128,128]{1,0:T(8,128)S(1)} custom-call(f32[128,128]{1,0:T(8,128)S(1)} %convolution_subtract_fusion.8), custom_call_target="Cholesky" | custom-call | tf_op jit(solution)/shard_map/jit(cholesky)/cholesky | solution.py:48
  307.6 0.6 compare_reduce_fusion
  310.8 0.3 fusion.10
  311.0 8.0 %while.4 = (s32[]{:T(128)}, f32[512,512]{1,0:T(8,128)S(1)}, s32[4,2]{0,1:T(2,128)S(1)}, f32[4,128,128]{2,1,0:T(8,128)S(1)}, s32[]{:T(128)}) while((s32[]{:T(128)}, f32[512,512]{1,0:T(8,128)S(1)}, s32[4,2]{0,1:T(2,128)S(1)}, f32[4,128,128]{2,1,0:T(8,128)S(1)}, s32[]{:T(128)}) %tuple.41), condition=%wide.while_cond.clone, body=%wide.while_body.clone.sunk | while | flops 2 | bytes 131181 | solution.py:50
  311.0 0.1 constant_dynamic-slice_fusion.2
  311.1 0.5 fusion.75
  311.6 1.4 bitcast_dynamic-update-slice_fusion.2
  313.0 0.1 constant_dynamic-slice_fusion.2
  313.1 0.5 fusion.75
  313.6 1.4 bitcast_dynamic-update-slice_fusion.2
  315.0 0.1 constant_dynamic-slice_fusion.2
  315.1 0.5 fusion.75
  315.6 1.4 bitcast_dynamic-update-slice_fusion.2
  317.1 0.1 constant_dynamic-slice_fusion.2
  317.1 0.5 fusion.75
  317.6 1.4 bitcast_dynamic-update-slice_fusion.2
  319.0 39.3 %custom-call.35 = f32[4,128,128]{1,2,0:T(8,128)S(1)} custom-call(f32[4,128,128]{2,1,0:T(8,128)S(1)} %get-tuple-element.18), custom_call_target="InvertDiagBlocksLowerTriangular" | custom-call | tf_op jit(solution)/shard_map/jit(_solve_triangular)/triangular_solve | solution.py:50
  358.4 1.3 broadcast_multiply_fusion
  359.7 0.4 fusion.30
  360.2 0.6 convolution_subtract_fusion.3
  360.8 0.4 fusion.48
  361.2 1.0 convolution_subtract_fusion.2
  362.2 0.4 fusion.50
  362.6 1.5 convolution_subtract_fusion.5
  364.1 0.4 fusion.52
  364.5 0.1 maximum_bitcast_fusion
  364.6 0.4 fusion.28
  365.1 0.6 convolution_subtract_fusion.1
  365.7 0.4 fusion.47
  366.1 1.0 convolution_subtract_fusion
  367.1 0.4 fusion.49
  367.5 1.5 convolution_subtract_fusion.4
  369.0 0.4 fusion.51
  369.5 1.3 copy.7
  370.8 1.3 copy.6
  (14 shorter events, 0.3 us)
Async XLA Ops:
  7.2 216.1 %all-reduce.4.cloned.1.call-start = ((), (), s32[]{:S(2)}) async-start(), calls=%async_computation | async-start | bytes 4194304 | tf_op jit(solution)/shard_map/psum | solution.py:47
  8.7 39.3 %collective-permute-start = (f32[3073,128]{1,0:T(8,128)S(1)}, f32[3073,128]{1,0:T(8,128)S(1)}, u32[]{:S(2)}, u32[]{:S(2)}) collective-permute-start(f32[3073,128]{1,0:T(8,128)S(1)} %slice.124), channel_id=1, source_target_pairs={{1,0},{2,1},{3,2},{4,3},{5,4},{6,5},{7,6},{8,7},{9,8},{10,9},{11,1... | collective-permute-start | bytes 4720136 | tf_op jit(solution)/shard_map/ppermute | solution.py:13
Sparse Core Ops, SparseCore 0:
  83.9 139.3 all-reduce.3
where the time goes:
time: 384 us; the launch traced here: 379 us
  waiting for transfers between devices  176 us (46%)
  other arithmetic  125 us (33%)
  matrix products  45 us (12%)
  between operations  17.1 us (4%)
  local copies, waits for them, and re-layouts  14.9 us (4%)
    psum x1, waiting for transfers between devices, on_device(): gram, cross = lax.psum((gram, cross), ('grp', 'span'))  140 us
    another operation x15, other arithmetic, on_device(): lower = jnp.linalg.cholesky(gram * scale)  79.7 us
    another operation x4, other arithmetic, on_device(): operator = jax.scipy.linalg.solve_triangular(lower, middle.T, lower=True).T  39.6 us
    ppermute x1, waiting for transfers between devices, shifted(): lax.ppermute(value, axis, [(source, source + steps) for source in range(l...  36.3 us
    dot_general x2, matrix products, inner_rows(): lax.dot_general(left, right, (((0,), (0,)), ((), ())), precision=lax.Prec...  33.6 us
    another operation x13, local copies, waits for them, and re-layouts, on_device(): operator = jax.scipy.linalg.solve_triangular(lower, middle.T, lower=True).T  7.92 us
  transfers between devices with their start and end apart: 2, of which 2 were waited for; matrix products, arithmetic and copies ran while one was open for 0% of the time, Pallas kernels for 0%

commit v1 on v0

--- a/solution.py
+++ b/solution.py
@@ -44,7 +44,7 @@
     cross = inner_rows(head * inside[:, None], hank[1 : count + 1])
     scale = 1.0 / last_row
     gram = inner_rows(weighted, head)
-    gram, cross = lax.psum((gram, cross), ("grp", "span"))
+    gram, cross = lax.psum(lax.psum((gram, cross), "grp"), "span")
     lower = jnp.linalg.cholesky(gram * scale)
     middle = jax.scipy.linalg.solve_triangular(lower, cross * scale, lower=True)
     operator = jax.scipy.linalg.solve_triangular(lower, middle.T, lower=True).T

time: 384 us -> 407 us (1.060)
  waiting for transfers between devices: 176 us -> 199 us
    psum x1 -> x2, waiting for transfers between devices: 140 us -> 162 us  [on_device(): gram, cross = lax.psum(lax.psum((gram, cross), 'grp'), 'span')]
  transfers between devices with their start and end apart: 2 -> 3, of which waited for: 2 -> 3; matrix products, arithmetic and copies ran while one was open for 0% -> 0% of each run, Pallas kernels for 0% -> 0%
where the time goes in v1:
time: 407 us; the launch traced here: 402 us
  waiting for transfers between devices  199 us (49%)
  other arithmetic  125 us (31%)
  matrix products  45.2 us (11%)
  between operations  17.2 us (4%)
  local copies, waits for them, and re-layouts  14.9 us (4%)
    psum x2, waiting for transfers between devices, on_device(): gram, cross = lax.psum(lax.psum((gram, cross), 'grp'), 'span')  162 us
    another operation x15, other arithmetic, on_device(): lower = jnp.linalg.cholesky(gram * scale)  79.4 us
    another operation x4, other arithmetic, on_device(): operator = jax.scipy.linalg.solve_triangular(lower, middle.T, lower=True).T  39.6 us
    ppermute x1, waiting for transfers between devices, shifted(): lax.ppermute(value, axis, [(source, source + steps) for source in range(l...  36.3 us
    dot_general x2, matrix products, inner_rows(): lax.dot_general(left, right, (((0,), (0,)), ((), ())), precision=lax.Prec...  33.8 us
  transfers between devices with their start and end apart: 3, of which 3 were waited for; matrix products, arithmetic and copies ran while one was open for 0% of the time, Pallas kernels for 0%

profile of v1, /device:TPU:0, one launch (start us, length us, event | category | flops | bytes accessed | tf_op | source)
XLA Modules:
  0.0 401.9 jit_solution(15200298157195339105)
XLA Ops:
  7.2 1.5 slice.124
  8.7 1.3 collective-permute-start
  10.0 1.7 constant_dynamic-update-slice_fusion.1
  11.8 36.3 %collective-permute-done = f32[3073,128]{1,0:T(8,128)S(1)} collective-permute-done((f32[3073,128]{1,0:T(8,128)S(1)}, f32[3073,128]{1,0:T(8,128)S(1)}, u32[]{:S(2)}, u32[]{:S(2)}) %collective-permute-start) | collective-permute-done | bytes 1573408 | tf_op jit(solution)/shard_map/ppermute | solution.py:13
  48.1 0.1 constant_dynamic-update-slice_fusion
  48.2 0.5 fusion.64
  48.7 1.4 pad_maximum_fusion
  50.1 17.3 %fusion.2 = f32[512,512]{0,1:T(8,128)} fusion(f32[4097,512]{1,0:T(8,128)S(1)} %pad_maximum_fusion, f32[4096]{0:T(1024)S(1)} %get-tuple-element.54), kind=kOutput, calls=%fused_computation.5 | convolution fusion | flops 12886999040 | bytes 17842176 | tf_op jit(solution)/shard_map/dot_general | solution.py:17
  67.4 16.5 %fusion = f32[512,512]{0,1:T(8,128)} fusion(f32[4097,512]{1,0:T(8,128)S(1)} %pad_maximum_fusion, f32[4096]{0:T(1024)S(1)} %get-tuple-element.53), kind=kOutput, calls=%fused_computation.2 | convolution fusion | flops 12886999040 | bytes 17842176 | tf_op jit(solution)/shard_map/dot_general | solution.py:17
  84.0 56.2 %all-reduce.8.cloned.1.call-done = (f32[512,512]{0,1:T(8,128)}, f32[512,512]{0,1:T(8,128)}) async-done(((f32[512,512]{0,1:T(8,128)}, f32[512,512]{0,1:T(8,128)}), (f32[512,512]{0,1:T(8,128)}, f32[512,512]{0,1:T(8,128)})) %all-reduce.8.cloned.1.call-update) | async-done | bytes 2097168 | tf_op jit(solution)/shard_map/psum | solution.py:47
  140.3 106.0 %all-reduce.6.cloned.1.call-done = (f32[512,512]{0,1:T(8,128)}, f32[512,512]{0,1:T(8,128)}) async-done(((f32[512,512]{0,1:T(8,128)}, f32[512,512]{0,1:T(8,128)}), (f32[512,512]{0,1:T(8,128)}, f32[512,512]{0,1:T(8,128)})) %all-reduce.6.cloned.1.call-update) | async-done | bytes 2097168 | tf_op jit(solution)/shard_map/psum | solution.py:47
  246.3 1.3 broadcast_multiply_fusion.1
  247.6 0.3 copy.4
  248.0 1.5 fusion.9
  249.4 11.7 %cholesky.104 = f32[128,128]{1,0:T(8,128)S(1)} custom-call(f32[128,128]{1,0:T(8,128)S(1)} %cholesky.266), custom_call_target="Cholesky" | custom-call | tf_op jit(solution)/shard_map/jit(cholesky)/cholesky | solution.py:48
  261.2 0.1 cholesky.224
  261.3 9.8 %custom-call.30 = f32[1,128,128]{1,2,0:T(8,128)S(1)} custom-call(f32[1,128,128]{2,1,0:T(8,128)S(1)} %get-tuple-element.50), custom_call_target="InvertDiagBlocksLowerTriangular" | custom-call | tf_op jit(solution)/shard_map/jit(cholesky)/cholesky | solution.py:48
  271.1 0.3 constant_dynamic-update-slice_fusion.5
  271.5 0.3 convolution_subtract_fusion.6
  271.8 11.7 %cholesky.217 = f32[128,128]{1,0:T(8,128)S(1)} custom-call(f32[128,128]{1,0:T(8,128)S(1)} %cholesky.270), custom_call_target="Cholesky" | custom-call | tf_op jit(solution)/shard_map/jit(cholesky)/cholesky | solution.py:48
  283.6 0.6 compare_reduce_fusion.2
  284.2 0.6 compare_reduce_fusion.3
  284.8 9.9 %custom-call.31 = f32[1,128,128]{1,2,0:T(8,128)S(1)} custom-call(f32[1,128,128]{2,1,0:T(8,128)S(1)} %get-tuple-element.47), custom_call_target="InvertDiagBlocksLowerTriangular" | custom-call | tf_op jit(solution)/shard_map/jit(cholesky)/cholesky | solution.py:48
  294.8 0.3 convolution_dynamic-update-slice_fusion
  295.1 0.4 convolution_subtract_fusion.7
  295.5 11.7 %cholesky.238 = f32[128,128]{1,0:T(8,128)S(1)} custom-call(f32[128,128]{1,0:T(8,128)S(1)} %cholesky.275), custom_call_target="Cholesky" | custom-call | tf_op jit(solution)/shard_map/jit(cholesky)/cholesky | solution.py:48
  307.2 0.7 compare_reduce_fusion.1
  307.9 9.8 %custom-call.32 = f32[1,128,128]{1,2,0:T(8,128)S(1)} custom-call(f32[1,128,128]{2,1,0:T(8,128)S(1)} %get-tuple-element.44), custom_call_target="InvertDiagBlocksLowerTriangular" | custom-call | tf_op jit(solution)/shard_map/jit(cholesky)/cholesky | solution.py:48
  317.7 0.2 convolution_dynamic-update-slice_fusion.1
  317.9 0.4 convolution_subtract_fusion.8
  318.3 11.9 %cholesky.255 = f32[128,128]{1,0:T(8,128)S(1)} custom-call(f32[128,128]{1,0:T(8,128)S(1)} %convolution_subtract_fusion.8), custom_call_target="Cholesky" | custom-call | tf_op jit(solution)/shard_map/jit(cholesky)/cholesky | solution.py:48
  330.3 0.6 compare_reduce_fusion
  333.5 0.3 fusion.10
  333.7 8.0 %while.4 = (s32[]{:T(128)}, f32[512,512]{1,0:T(8,128)S(1)}, s32[4,2]{0,1:T(2,128)S(1)}, f32[4,128,128]{2,1,0:T(8,128)S(1)}, s32[]{:T(128)}) while((s32[]{:T(128)}, f32[512,512]{1,0:T(8,128)S(1)}, s32[4,2]{0,1:T(2,128)S(1)}, f32[4,128,128]{2,1,0:T(8,128)S(1)}, s32[]{:T(128)}) %tuple.41), condition=%wide.while_cond.clone, body=%wide.while_body.clone.sunk | while | flops 2 | bytes 131181 | solution.py:50
  333.8 0.1 constant_dynamic-slice_fusion.2
  333.8 0.5 fusion.75
  334.4 1.4 bitcast_dynamic-update-slice_fusion.2
  335.8 0.1 constant_dynamic-slice_fusion.2
  335.8 0.5 fusion.75
  336.4 1.4 bitcast_dynamic-update-slice_fusion.2
  337.8 0.1 constant_dynamic-slice_fusion.2
  337.8 0.5 fusion.75
  338.4 1.4 bitcast_dynamic-update-slice_fusion.2
  339.8 0.1 constant_dynamic-slice_fusion.2
  339.8 0.5 fusion.75
  340.4 1.4 bitcast_dynamic-update-slice_fusion.2
  341.8 39.3 %custom-call.35 = f32[4,128,128]{1,2,0:T(8,128)S(1)} custom-call(f32[4,128,128]{2,1,0:T(8,128)S(1)} %get-tuple-element.18), custom_call_target="InvertDiagBlocksLowerTriangular" | custom-call | tf_op jit(solution)/shard_map/jit(_solve_triangular)/triangular_solve | solution.py:50
  381.1 1.3 broadcast_multiply_fusion
  382.4 0.4 fusion.30
  382.9 0.6 convolution_subtract_fusion.3
  383.5 0.4 fusion.48
  383.9 1.0 convolution_subtract_fusion.2
  384.9 0.4 fusion.50
  385.3 1.5 convolution_subtract_fusion.5
  386.8 0.4 fusion.52
  387.3 0.4 fusion.28
  387.8 0.6 convolution_subtract_fusion.1
  388.4 0.4 fusion.47
  388.8 1.0 convolution_subtract_fusion
  389.8 0.4 fusion.49
  390.2 1.5 convolution_subtract_fusion.4
  391.7 0.4 fusion.51
  392.2 1.3 copy.7
  393.5 1.3 copy.6
  (17 shorter events, 0.4 us)
Async XLA Ops:
  7.2 133.1 %all-reduce.8.cloned.1.call-start = ((), (), s32[]{:S(2)}) async-start(), calls=%async_computation.1 | async-start | bytes 4194304 | tf_op jit(solution)/shard_map/psum | solution.py:47
  8.7 39.3 %collective-permute-start = (f32[3073,128]{1,0:T(8,128)S(1)}, f32[3073,128]{1,0:T(8,128)S(1)}, u32[]{:S(2)}, u32[]{:S(2)}) collective-permute-start(f32[3073,128]{1,0:T(8,128)S(1)} %slice.124), channel_id=1, source_target_pairs={{1,0},{2,1},{3,2},{4,3},{5,4},{6,5},{7,6},{8,7},{9,8},{10,9},{11,1... | collective-permute-start | bytes 4720136 | tf_op jit(solution)/shard_map/ppermute | solution.py:13
  83.9 162.3 %all-reduce.6.cloned.1.call-start = ((), (), s32[]{:S(2)}) async-start(), calls=%async_computation | async-start | bytes 4194304 | tf_op jit(solution)/shard_map/psum | solution.py:47
Sparse Core Ops, SparseCore 0:
  84.1 56.1 all-reduce.7
  143.9 102.3 all-reduce.5
